TPU v7x, 512 devices: a whole 4x4x16 slice. The times are simulated.
512 devices in a mesh: tm: 16 (over z), expert: 32 (over x, y, core).
Axes of the slice: x: 4, y: 4, z: 16, core: 2. Of those that a mesh axis runs over, the one named last changes fastest.
Arguments:
- x_in: float32 [32, 4096, 1024], P('expert', 'tm'), may hold values from -6 to 6
- z_gate: bfloat16 [32, 4096, 1024], P('expert', 'tm'), may hold values from -6 to 6
- b_proj: float32 [32, 4096, 128], P('expert', 'tm'), may hold values from -1.5 to 1.5
- c_proj: float32 [32, 4096, 128], P('expert', 'tm'), may hold values from -1.5 to 1.5
- decay_log: float32 [32, 4096, 16], P('expert', 'tm'), as said below
- skip_gain: float32 [16], replicated, may hold values from 0.5 to 2
- residual: float32 [32, 4096, 1024], P('expert', 'tm'), may hold values from -6 to 6
- ssd_gain: float32 [1024], replicated, may hold values from 0.5 to 1.5
- moe_gain: float32 [1024], replicated, may hold values from 0.5 to 1.5
- w_gate: bfloat16 [32, 1024, 1536], P('expert', 'tm'), may hold values from -0.1875 to 0.1875
- w_up: bfloat16 [32, 1024, 1536], P('expert', 'tm'), may hold values from -0.1875 to 0.1875
- w_down: bfloat16 [32, 1536, 1024], P('expert', 'tm'), may hold values from -0.15625 to 0.15625
- routes: int32 [32, 4096, 2], P('expert', 'tm'), may hold values from 0 to 31, all different within a row; in each aligned block of 256 rows (0 to 255, 256 to 511, ..., all dimensions but the last counted through in order) at most 24 rows name the same one
- route_weights: float32 [32, 4096, 2], P('expert', 'tm'), may hold values from 0.2 to 1
Outputs:
- mixed: float32 [32, 4096, 1024], P('expert', 'tm')
Inputs may be any that keep to these rules, and one draw needn't show every extreme that they name: `routes`: the two experts of a time step differ. Among the time steps of one device no expert is named more than 24 times, and in every draw some device names some expert exactly 24 times. `decay_log`: every entry is at most zero.
All inputs are finite; a program needn't handle non-finite values.
Results may differ from a plain program's by a relative error of at most 0.0021.
Values may be sent and summed in bfloat16 or wider, within the bound.
No kernel may reach another device: no remote copies, remote signals or barrier semaphores. Data moves between devices by JAX's collectives and lax.ppermute only.
A program may use at most 64 MiB of HBM per device.

v0:
```python
import math
import jax
import jax.numpy as jnp
from jax import lax
from jax.sharding import PartitionSpec as P

exact_mode = lax.Precision.HIGHEST


def carried_in_2(value, axis, join, neutral):
    count, mine = (lax.axis_size(axis), lax.axis_index(axis))
    pieces = jax.tree.map(lambda part: lax.all_gather(part, axis), value)
    running = jax.tree.map(
        lambda part, zero: jnp.full_like(part, 0) + jnp.asarray(zero, part.dtype), value, neutral
    )

    def lap(position, running):
        longer = join(running, jax.tree.map(lambda part: part[position], pieces))
        return jax.tree.map(lambda new, old: jnp.where(position < mine, new, old), longer, running)

    return lax.fori_loop(0, count - 1, lap, running)


def group_carry(state, values, b_rows, running):
    remains = jnp.exp(running[-1][None, :] - running)
    fresh = jnp.einsum("jhp,jn->hpn", values * remains[:, :, None], b_rows, precision=exact_mode)
    return jnp.exp(running[-1])[:, None, None] * state + fresh


def group_step(state, inputs, skip_gain):
    values, b_rows, c_rows, log_rates = inputs
    length = values.shape[0]
    running = jnp.cumsum(log_rates, axis=0)
    across = running.T[:, :, None] - running.T[:, None, :]
    places = jnp.arange(length)
    causal = (places[:, None] >= places[None, :])[None]
    masked = jnp.where(causal, jnp.exp(jnp.where(causal, across, 0.0)), 0.0)
    scores = jnp.dot(c_rows, b_rows.T, precision=exact_mode)
    mixing = masked * scores[None]
    output = jnp.einsum("hij,jhp->ihp", mixing, values, precision=exact_mode)
    output = output + jnp.exp(running)[:, :, None] * jnp.einsum(
        "in,hpn->ihp", c_rows, state, precision=exact_mode
    )
    output = output + skip_gain[None, :, None] * values
    return (group_carry(state, values, b_rows, running), output)


def incoming_state(through, local_end):

    def combine(earlier, later):
        return (earlier[0] * later[0], later[0][:, None, None] * earlier[1] + later[1])

    prefix = carried_in_2(
        (through, local_end), "tm", combine, (jnp.ones_like(through), jnp.zeros_like(local_end))
    )
    return prefix[1]


def rms_scale(rows, gain):
    return gain * rows / jnp.sqrt(jnp.mean(rows * rows, axis=-1, keepdims=True) + 1e-05)


def per_device(
    x_in,
    z_gate,
    b_proj,
    c_proj,
    decay_log,
    skip_gain,
    residual,
    ssd_gain,
    moe_gain,
    w_gate,
    w_up,
    w_down,
    routes,
    route_weights,
):
    heads = skip_gain.shape[0]
    model_width = x_in.shape[2]
    width = model_width // heads
    length = x_in.shape[1]
    block = math.gcd(length, 256)
    count = length // block
    values = x_in[0].reshape(length, heads, width)
    b_rows = b_proj[0]
    c_rows = c_proj[0]
    log_rates = decay_log[0]
    inputs = (
        values.reshape(count, block, heads, width),
        b_rows.reshape(count, block, -1),
        c_rows.reshape(count, block, -1),
        log_rates.reshape(count, block, heads),
    )
    start = jnp.zeros((heads, width, b_rows.shape[1]), jnp.float32)
    through = jnp.exp(jnp.sum(log_rates, axis=0))
    local_end, outputs = lax.scan(
        lambda state, piece: group_step(state, piece, skip_gain), start, inputs
    )
    incoming = incoming_state(through, local_end)
    running = jnp.cumsum(log_rates, axis=0)
    carried_in = jnp.exp(running)[:, :, None] * jnp.einsum(
        "in,hpn->ihp", c_rows, incoming, precision=exact_mode
    )
    mixed_ssd = (outputs.reshape(length, heads, width) + carried_in).reshape(length, model_width)
    gated = mixed_ssd * jax.nn.silu(z_gate[0].astype(jnp.float32))
    hres = residual[0] + rms_scale(gated, ssd_gain)
    normed = rms_scale(hres, moe_gain).astype(jnp.bfloat16)
    expert_count = lax.axis_size("expert")
    capacity = max(2, 3 * length // expert_count)
    flat_routes = routes[0].reshape(-1)
    picked_one = (flat_routes[:, None] == jnp.arange(expert_count)[None, :]).astype(jnp.int32)
    earlier_hits = jnp.cumsum(picked_one, axis=0) - picked_one
    slot_index = jnp.sum(earlier_hits * picked_one, axis=1)
    target = flat_routes * capacity + slot_index
    repeated = jnp.broadcast_to(normed[:, None, :], (length, 2, model_width)).reshape(
        2 * length, model_width
    )
    outgoing = (
        jnp.zeros((expert_count * capacity, model_width), jnp.bfloat16).at[target].set(repeated)
    )
    received = lax.all_to_all(
        outgoing.reshape(expert_count, capacity, model_width),
        "expert",
        split_axis=0,
        concat_axis=0,
        tiled=True,
    )
    received = received.reshape(expert_count * capacity, model_width)
    slot_rows = expert_count * capacity
    columns = received
    gate = jnp.dot(
        columns,
        lax.all_gather(w_gate[0], "tm", axis=0, tiled=True),
        preferred_element_type=jnp.float32,
    )
    upper = jnp.dot(
        columns,
        lax.all_gather(w_up[0], "tm", axis=0, tiled=True),
        preferred_element_type=jnp.float32,
    )
    hidden = (jax.nn.silu(gate) * upper).astype(jnp.bfloat16)
    columns = hidden
    produced = jnp.dot(
        columns,
        lax.all_gather(w_down[0], "tm", axis=0, tiled=True),
        preferred_element_type=jnp.float32,
    ).astype(jnp.bfloat16)
    back = lax.all_to_all(
        produced.reshape(expert_count, capacity, model_width),
        "expert",
        split_axis=0,
        concat_axis=0,
        tiled=True,
    )
    back = back.reshape(slot_rows, model_width)
    fetched = back[target].astype(jnp.float32).reshape(length, 2, model_width)
    weights_here = route_weights[0]
    moe = fetched[:, 0, :] * weights_here[:, 0:1] + fetched[:, 1, :] * weights_here[:, 1:2]
    return (hres + moe).reshape(1, length, model_width)


def solution(mesh):
    in_specs = (
        P("expert", "tm", None),
        P("expert", "tm", None),
        P("expert", "tm", None),
        P("expert", "tm", None),
        P("expert", "tm", None),
        P(),
        P("expert", "tm", None),
        P(),
        P(),
        P("expert", "tm", None),
        P("expert", "tm", None),
        P("expert", "tm", None),
        P("expert", "tm", None),
        P("expert", "tm", None),
    )
    out_specs = P("expert", "tm", None)
    return jax.shard_map(
        per_device, mesh=mesh, in_specs=in_specs, out_specs=out_specs, check_vma=False
    )
```

profile of v0, /device:TPU:1, one launch (start us, length us, event | category | flops | bytes accessed | tf_op | source)
XLA Modules:
  0.0 405.9 jit_solution(9429766804105325587)
XLA Ops:
  8.5 1.6 copy.54
  10.2 1.8 convolution_add_fusion
  17.1 32.2 %all-reduce = f32[256]{0:T(256)S(1)} all-reduce(f32[256]{0:T(256)S(1)} %exponential_dynamic-update-slice_fusion), channel_id=2, replica_groups=mesh['tm'=16,'expert'=32] {'tm'}, use_global_device_ids=true, to_apply=%add | all-reduce | flops 256 | bytes 2048
  52.4 5.1 %fusion.24 = f32[256,16,64]{0,2,1:T(8,128)S(1)} fusion(f32[256,16,64]{0,2,1:T(8,128)S(1)} %bitcast.161, f32[256,256]{1,0:T(8,128)S(1)} %fusion.49, f32[16,256]{1,0:T(8,128)S(1)} %get-tuple-element.159, pred[256,256]{1,0:T(8,128)(4,1)S(1)} %iota_compare_fusion), kind=kOutput, calls=%fused_computation.23 | convolution fusion | flops 809500672 | bytes 2441216 | tf_op jit(solution)/shard_map/while/body/eval_jaxpr/hij,jhp->ihp/dot_general | solution.py:40
  57.6 2.1 fusion.31
  59.7 64.1 %all-gather.10.cloned.1.call-done = f32[256,64,128]{2,1,0:T(8,128)} async-done(((f32[16,64,128]{2,1,0:T(8,128)}), f32[256,64,128]{2,1,0:T(8,128)}) %all-gather.10.cloned.1.call-update) | async-done | bytes 8388624 | tf_op jit(solution)/shard_map/all_gather | solution.py:12
  123.7 18.2 %while.9 = (s32[]{:T(128)}, f32[16,64,128]{2,1,0:T(8,128)S(1)}, s32[]{:T(128)}, f32[16,16]{1,0:T(8,128)S(1)}, f32[16,16,64,128]{3,2,1,0:T(8,128)}, /*index=5*/s32[]{:T(128)}, s32[]{:T(128)}) while((s32[]{:T(128)}, f32[16,64,128]{2,1,0:T(8,128)S(1)}, s32[]{:T(128)}, f32[16,16]{1,0:T(8,128)S(1)}, f32[16,16,64,128]{3,2,1,0:T(8,128)}, ...), condition=%wide.region_4.5_spmd.clone, body=%wide.region_3.4_spmd.clone.sunk | while | flops 524292 | bytes 1573161 | solution.py:21
  142.0 2.8 multiply_reduce_fusion.1
  144.8 1.3 copy.62
  146.1 1.8 multiply_reduce_fusion
  149.9 4.5 %scatter_custom_fusion = bf16[768,1024]{1,0:T(8,128)(2,1)} fusion(s32[512]{0:T(512)S(1)} %bitcast.171, bf16[512,1024]{1,0:T(8,128)(2,1)} %reshape.351, bf16[]{:T(256)} %constant.72.clone.1), kind=kCustom, calls=%fused_computation.51 | custom fusion | bytes 1573376 | tf_op jit(solution)/shard_map/scatter | solution.py:120
  154.4 7.5 %all-to-all-start = ((bf16[32,24,1024]{2,1,0:T(8,128)(2,1)}), bf16[32,24,1024]{2,1,0:T(8,128)(2,1)S(1)}, u32[]{:S(2)}, u32[]{:S(2)}) async-start(bf16[32,24,1024]{2,1,0:T(8,128)(2,1)} %bitcast.23), calls=%async_computation | async-start | bytes 3145728 | tf_op jit(solution)/shard_map/all_to_all | solution.py:122
  162.0 29.4 %all-gather.12.cloned.1.call-done = bf16[1,1024,1536]{2,1,0:T(8,128)(2,1)} async-done(((bf16[1,64,1536]{2,1,0:T(8,128)(2,1)}), bf16[1,1024,1536]{2,1,0:T(8,128)(2,1)}) %all-gather.12.cloned.1.call-update) | async-done | bytes 3145744 | tf_op jit(solution)/shard_map/all_gather | solution.py:134
  191.3 6.1 %fusion.10 = f32[768,1536]{1,0:T(8,128)} fusion(bf16[768,1024]{1,0:T(8,128)(2,1)S(1)} %bitcast.166, bf16[1,1024,1536]{2,1,0:T(8,128)(2,1)} %all-gather.12.cloned.1.call-done), kind=kOutput, calls=%fused_computation.15 | convolution fusion | flops 2415919104 | bytes 9437184 | tf_op jit(solution)/shard_map/dot_general | solution.py:132
  197.4 69.0 %all-gather.14.cloned.1.call-done = bf16[1,1024,1536]{2,1,0:T(8,128)(2,1)} async-done(((bf16[1,64,1536]{2,1,0:T(8,128)(2,1)}), bf16[1,1024,1536]{2,1,0:T(8,128)(2,1)}) %all-gather.14.cloned.1.call-update) | async-done | bytes 3145744 | tf_op jit(solution)/shard_map/all_gather | solution.py:139
  266.4 75.2 %all-gather.16.cloned.1.call-done = bf16[1,1536,1024]{2,1,0:T(8,128)(2,1)} async-done(((bf16[1,96,1024]{2,1,0:T(8,128)(2,1)}), bf16[1,1536,1024]{2,1,0:T(8,128)(2,1)}) %all-gather.16.cloned.1.call-update) | async-done | bytes 3145744 | tf_op jit(solution)/shard_map/all_gather | solution.py:146
  341.6 10.5 %fusion.19 = bf16[768,1024]{1,0:T(8,128)(2,1)} fusion(bf16[1,1536,1024]{2,1,0:T(8,128)(2,1)} %all-gather.16.cloned.1.call-done, f32[768,1536]{1,0:T(8,128)} %fusion.10, bf16[768,1024]{1,0:T(8,128)(2,1)S(1)} %bitcast.167, bf16[1,1024,1536]{2,1,0:T(8,128)(2,1)} %all-gather.14.cloned.1.call-done), kind=kOutput, calls=%fused_computation.22 | convolution fusion | flops 4839702528 | bytes 14155776 | tf_op jit(solution)/shard_map/dot_general | solution.py:144
  352.0 16.2 %all-to-all-start.1 = ((bf16[32,24,1024]{2,1,0:T(8,128)(2,1)}), bf16[32,24,1024]{2,1,0:T(8,128)(2,1)S(1)}, u32[]{:S(2)}, u32[]{:S(2)}) async-start(bf16[32,24,1024]{2,1,0:T(8,128)(2,1)} %bitcast.168), calls=%async_computation.1 | async-start | bytes 3145728 | tf_op jit(solution)/shard_map/all_to_all | solution.py:149
  368.3 1.3 copy.56
  369.6 21.3 %all-to-all-done.1 = bf16[32,24,1024]{2,1,0:T(8,128)(2,1)S(1)} async-done(((bf16[32,24,1024]{2,1,0:T(8,128)(2,1)}), bf16[32,24,1024]{2,1,0:T(8,128)(2,1)S(1)}, u32[]{:S(2)}, u32[]{:S(2)}) %all-to-all-start.1) | async-done | bytes 1572896 | tf_op jit(solution)/shard_map/all_to_all | solution.py:149
  390.9 2.8 gather_fusion
  393.7 2.4 reshape.338
  396.1 1.6 fusion.61
  397.7 1.6 fusion.34
  (102 shorter events, 29.2 us)
Async XLA Ops:
  6.5 8.1 %copy-start = (f32[1,256,128]{2,1,0:T(8,128)S(1)}, f32[1,256,128]{2,1,0:T(8,128)}, u32[]{:S(2)}) copy-start(f32[1,256,128]{2,1,0:T(8,128)} %param.19) | copy-start | bytes 393220
  6.5 3.6 copy-start.5
  6.5 117.2 %all-gather.10.cloned.1.call-start = ((), (), s32[]{:S(2)}) async-start(), calls=%async_computation.2 | async-start | bytes 8912896 | tf_op jit(solution)/shard_map/all_gather | solution.py:12
  8.4 5.6 %copy-start.6 = (f32[1,256,16]{1,2,0:T(8,128)S(1)}, f32[1,256,16]{1,2,0:T(8,128)}, u32[]{:S(2)}) copy-start(f32[1,256,16]{1,2,0:T(8,128)} %param.20) | copy-start | bytes 49156
  8.5 5.7 %copy-start.8 = (s32[1,256,2]{1,2,0:T(2,128)S(1)}, s32[1,256,2]{1,2,0:T(2,128)}, u32[]{:S(2)}) copy-start(s32[1,256,2]{1,2,0:T(2,128)} %param.28) | copy-start | bytes 6148
  10.0 39.4 %copy-start.1 = (bf16[1,256,1024]{2,1,0:T(8,128)(2,1)S(1)}, bf16[1,256,1024]{2,1,0:T(8,128)(2,1)}, u32[]{:S(2)}) copy-start(bf16[1,256,1024]{2,1,0:T(8,128)(2,1)} %param.17) | copy-start | bytes 1572868
  12.0 179.4 %all-gather.12.cloned.1.call-start = ((), (), s32[]{:S(2)}) async-start(), calls=%async_computation.3 | async-start | bytes 3342336 | tf_op jit(solution)/shard_map/all_gather | solution.py:134
  12.7 253.7 %all-gather.14.cloned.1.call-start = ((), (), s32[]{:S(2)}) async-start(), calls=%async_computation.4 | async-start | bytes 3342336 | tf_op jit(solution)/shard_map/all_gather | solution.py:139
  13.4 328.1 %all-gather.16.cloned.1.call-start = ((), (), s32[]{:S(2)}) async-start(), calls=%async_computation.5 | async-start | bytes 3342336 | tf_op jit(solution)/shard_map/all_gather | solution.py:146
  52.4 5.1 %copy-start.11 = (f32[16]{0:T(128)S(1)}, f32[16]{0:T(128)}, u32[]{:S(2)}) copy-start(f32[16]{0:T(128)} %param.21) | copy-start | bytes 196
  142.0 4.2 %copy-start.3 = (f32[1,256,1024]{2,1,0:T(8,128)S(1)}, f32[1,256,1024]{2,1,0:T(8,128)}, u32[]{:S(2)}) copy-start(f32[1,256,1024]{2,1,0:T(8,128)} %param.22) | copy-start | bytes 3145732
  142.0 4.1 %copy-start.7 = (f32[1024]{0:T(1024)S(1)}, f32[1024]{0:T(1024)}, u32[]{:S(2)}) copy-start(f32[1024]{0:T(1024)} %param.23) | copy-start | bytes 12292
  144.8 3.1 copy-start.9
  154.4 36.9 %all-to-all-start = ((bf16[32,24,1024]{2,1,0:T(8,128)(2,1)}), bf16[32,24,1024]{2,1,0:T(8,128)(2,1)S(1)}, u32[]{:S(2)}, u32[]{:S(2)}) async-start(bf16[32,24,1024]{2,1,0:T(8,128)(2,1)} %bitcast.23), calls=%async_computation | async-start | bytes 3145728 | tf_op jit(solution)/shard_map/all_to_all | solution.py:122
  352.0 16.2 %copy-start.10 = (f32[1,256,2]{1,2,0:T(2,128)S(1)}, f32[1,256,2]{1,2,0:T(2,128)}, u32[]{:S(2)}) copy-start(f32[1,256,2]{1,2,0:T(2,128)} %param.29) | copy-start | bytes 6148
  352.0 38.9 %all-to-all-start.1 = ((bf16[32,24,1024]{2,1,0:T(8,128)(2,1)}), bf16[32,24,1024]{2,1,0:T(8,128)(2,1)S(1)}, u32[]{:S(2)}, u32[]{:S(2)}) async-start(bf16[32,24,1024]{2,1,0:T(8,128)(2,1)} %bitcast.168), calls=%async_computation.1 | async-start | bytes 3145728 | tf_op jit(solution)/shard_map/all_to_all | solution.py:149
  396.1 1.7 copy-start.2
  396.1 1.7 copy-start.4
Sparse Core Ops, SparseCore 0:
  12.1 111.6 all-gather.9
  125.8 65.4 all-gather.11
  193.4 72.9 all-gather.13
  268.3 73.2 all-gather.15
where the time goes:
time: 407 us; the launch traced here: 406 us
  waiting for transfers between devices  261 us (64%)
  blocking collectives  32.2 us (8%)
  matrix products  28.7 us (7%)
  starting transfers between devices  23.9 us (6%)
  other arithmetic  23.6 us (6%)
  local copies, waits for them, and re-layouts  22.1 us (5%)
  between operations  14.1 us (3%)
    all_gather x1, waiting for transfers between devices, per_device(): lax.all_gather(w_down[0], 'tm', axis=0, tiled=True)  75.2 us
    all_gather x1, waiting for transfers between devices, per_device(): lax.all_gather(w_up[0], 'tm', axis=0, tiled=True)  69 us
    all_gather x1, waiting for transfers between devices, carried_in_2(): pieces = jax.tree.map(lambda part: lax.all_gather(part, axis), value)  64.1 us
    unnamed x1, blocking collectives  32.2 us
    all_gather x1, waiting for transfers between devices, per_device(): lax.all_gather(w_gate[0], 'tm', axis=0, tiled=True)  29.4 us
    all_to_all x1, waiting for transfers between devices, per_device(): lax.all_to_all(produced.reshape(expert_count, capacity, model_width), 'ex...  21.3 us
    select_n x15, other arithmetic, lap(): jnp.where(position < mine, new, old)  17.6 us
    all_to_all x1, starting transfers between devices, per_device(): lax.all_to_all(produced.reshape(expert_count, capacity, model_width), 'ex...  16.2 us
  transfers between devices with their start and end apart: 6, of which 5 were waited for; matrix products, arithmetic and copies ran while one was open for 12% of the time, Pallas kernels for 0%

commit v1 on v0

--- a/solution.py
+++ b/solution.py
@@ -5,6 +5,22 @@
 from jax.sharding import PartitionSpec as P
 
 exact_mode = lax.Precision.HIGHEST
+
+
+def collect(x, axis, dim):
+    ways, here, step = (lax.axis_size(axis), lax.axis_index(axis), x.shape[dim])
+    shape = [n * ways if d == dim else n for d, n in enumerate(x.shape)]
+    full = lax.dynamic_update_slice_in_dim(jnp.zeros(shape, x.dtype), x, here * step, axis=dim)
+    going_up = going_down = x
+    for far in range(1, ways // 2 + 1):
+        going_up = lax.ppermute(going_up, axis, [(d, (d + 1) % ways) for d in range(ways)])
+        full = lax.dynamic_update_slice_in_dim(full, going_up, (here - far) % ways * step, axis=dim)
+        if 2 * far < ways:
+            going_down = lax.ppermute(going_down, axis, [(d, (d - 1) % ways) for d in range(ways)])
+            full = lax.dynamic_update_slice_in_dim(
+                full, going_down, (here + far) % ways * step, axis=dim
+            )
+    return full
 
 
 def carried_in_2(value, axis, join, neutral):
@@ -134,11 +150,7 @@
         lax.all_gather(w_gate[0], "tm", axis=0, tiled=True),
         preferred_element_type=jnp.float32,
     )
-    upper = jnp.dot(
-        columns,
-        lax.all_gather(w_up[0], "tm", axis=0, tiled=True),
-        preferred_element_type=jnp.float32,
-    )
+    upper = jnp.dot(columns, collect(w_up[0], "tm", 0), preferred_element_type=jnp.float32)
     hidden = (jax.nn.silu(gate) * upper).astype(jnp.bfloat16)
     columns = hidden
     produced = jnp.dot(

time: 407 us -> 356 us (0.87)
  waiting for transfers between devices: 261 us -> 135 us
  starting transfers between devices: 23.9 us -> 78.6 us
  local copies, waits for them, and re-layouts: 22.1 us -> 47 us
  blocking collectives: 32.2 us -> 24.1 us
    all_gather x1 -> x0, waiting for transfers between devices: 69 us -> none  [per_device(): lax.all_gather(w_up[0], 'tm', axis=0, tiled=True)]
    ppermute x0 -> x15, starting transfers between devices: none -> 54.8 us  [the longest x7 37.1 us: collect(): lax.ppermute(going_down, axis, [(d, (d - 1) % ways) for d in range(ways)])]
    all_gather x1, waiting for transfers between devices: 64.1 us -> 20 us  [carried_in_2(): pieces = jax.tree.map(lambda part: lax.all_gather(part, axis), value)]
    ppermute x0 -> x15, waiting for transfers between devices: none -> 31.4 us  [the longest x8 31.4 us: collect(): lax.ppermute(going_up, axis, [(d, (d + 1) % ways) for d in range(ways)])]
    all_gather x1, waiting for transfers between devices: 29.4 us -> 0.01 us  [per_device(): lax.all_gather(w_gate[0], 'tm', axis=0, tiled=True)]
    all_gather x1, waiting for transfers between devices: 75.2 us -> 62.8 us  [per_device(): lax.all_gather(w_down[0], 'tm', axis=0, tiled=True)]
    dynamic_update_slice x0 -> x16, local copies, waits for them, and re-layouts: none -> 11.1 us  [the longest x8 5.59 us: collect(): lax.dynamic_update_slice_in_dim(full, going_up, (here - far) % ways * ste...]
    mul x15, local copies, waits for them, and re-layouts: 0.14 us -> 10.4 us  [combine(): later[0][:, None, None] * earlier[1] + later[1]]
  transfers between devices with their start and end apart: 6 -> 20, of which waited for: 5 -> 9; matrix products, arithmetic and copies ran while one was open for 12% -> 22% of each run, Pallas kernels for 0% -> 0%
where the time goes in v1:
time: 356 us; the launch traced here: 353 us
  waiting for transfers between devices  135 us (38%)
  starting transfers between devices  78.6 us (22%)
  local copies, waits for them, and re-layouts  47 us (13%)
  matrix products  29.7 us (8%)
  other arithmetic  24.1 us (7%)
  blocking collectives  24.1 us (7%)
  between operations  14.6 us (4%)
    all_gather x1, waiting for transfers between devices, per_device(): lax.all_gather(w_down[0], 'tm', axis=0, tiled=True)  62.8 us
    ppermute x7, starting transfers between devices, collect(): lax.ppermute(going_down, axis, [(d, (d - 1) % ways) for d in range(ways)])  37.1 us
    ppermute x8, waiting for transfers between devices, collect(): lax.ppermute(going_up, axis, [(d, (d + 1) % ways) for d in range(ways)])  31.4 us
    unnamed x1, blocking collectives  24.1 us
    all_to_all x1, waiting for transfers between devices, per_device(): lax.all_to_all(produced.reshape(expert_count, capacity, model_width), 'ex...  20.1 us
    all_gather x1, waiting for transfers between devices, carried_in_2(): pieces = jax.tree.map(lambda part: lax.all_gather(part, axis), value)  20 us
    ppermute x8, starting transfers between devices, collect(): lax.ppermute(going_up, axis, [(d, (d + 1) % ways) for d in range(ways)])  17.7 us
    select_n x15, other arithmetic, lap(): jnp.where(position < mine, new, old)  17.6 us
  transfers between devices with their start and end apart: 20, of which 9 were waited for; matrix products, arithmetic and copies ran while one was open for 22% of the time, Pallas kernels for 0%

profile of v1, /device:TPU:1, one launch (start us, length us, event | category | flops | bytes accessed | tf_op | source)
XLA Modules:
  0.0 353.5 jit_solution(11945313874773318110)
XLA Ops:
  12.8 4.4 %collective-permute-start = (bf16[64,1536]{1,0:T(8,128)(2,1)S(1)}, bf16[64,1536]{1,0:T(8,128)(2,1)S(1)}, u32[]{:S(2)}, u32[]{:S(2)}) collective-permute-start(bf16[64,1536]{1,0:T(8,128)(2,1)S(1)} %bitcast.167), channel_id=1, source_target_pairs={{0,32},{32,64},{64,96},{96,128},{128,160},{160,192},{192,224},{224... | collective-permute-start | bytes 589832 | tf_op jit(solution)/shard_map/ppermute | solution.py:16
  17.2 9.5 %collective-permute-start.1 = (bf16[64,1536]{1,0:T(8,128)(2,1)S(1)}, bf16[64,1536]{1,0:T(8,128)(2,1)S(1)}, u32[]{:S(2)}, u32[]{:S(2)}) collective-permute-start(bf16[64,1536]{1,0:T(8,128)(2,1)S(1)} %bitcast.168), channel_id=1, source_target_pairs={{0,480},{32,0},{64,32},{96,64},{128,96},{160,128},{192,160},{224,1... | collective-permute-start | bytes 589832 | tf_op jit(solution)/shard_map/ppermute | solution.py:19
  29.7 24.1 %all-reduce = f32[256]{0:T(256)S(1)} all-reduce(f32[256]{0:T(256)S(1)} %exponential_dynamic-update-slice_fusion), channel_id=2, replica_groups=mesh['tm'=16,'expert'=32] {'tm'}, use_global_device_ids=true, to_apply=%add | all-reduce | flops 256 | bytes 2048
  60.4 5.1 %fusion.19 = f32[256,16,64]{0,2,1:T(8,128)S(1)} fusion(f32[256,16,64]{0,2,1:T(8,128)S(1)} %bitcast.157, f32[256,256]{1,0:T(8,128)S(1)} %fusion.44, f32[16,256]{1,0:T(8,128)S(1)} %get-tuple-element.159, pred[256,256]{1,0:T(8,128)(4,1)S(1)} %iota_compare_fusion), kind=kOutput, calls=%fused_computation.22 | convolution fusion | flops 809500672 | bytes 2441216 | tf_op jit(solution)/shard_map/while/body/eval_jaxpr/hij,jhp->ihp/dot_general | solution.py:56
  70.1 4.6 %collective-permute-start.3 = (bf16[64,1536]{1,0:T(8,128)(2,1)S(1)}, bf16[64,1536]{1,0:T(8,128)(2,1)S(1)}, u32[]{:S(2)}, u32[]{:S(2)}) collective-permute-start(bf16[64,1536]{1,0:T(8,128)(2,1)S(1)} %collective-permute-done.1), channel_id=1, source_target_pairs={{0,480},{32,0},{64,32},{96,64},{128,96},{160,128},{192,160},{224,1... | collective-permute-start | bytes 589832 | tf_op jit(solution)/shard_map/ppermute | solution.py:19
  76.1 4.3 %collective-permute-done.2 = bf16[64,1536]{1,0:T(8,128)(2,1)S(1)} collective-permute-done((bf16[64,1536]{1,0:T(8,128)(2,1)S(1)}, bf16[64,1536]{1,0:T(8,128)(2,1)S(1)}, u32[]{:S(2)}, u32[]{:S(2)}) %collective-permute-start.2) | collective-permute-done | bytes 196640 | tf_op jit(solution)/shard_map/ppermute | solution.py:16
  82.3 4.6 %collective-permute-start.5 = (bf16[64,1536]{1,0:T(8,128)(2,1)S(1)}, bf16[64,1536]{1,0:T(8,128)(2,1)S(1)}, u32[]{:S(2)}, u32[]{:S(2)}) collective-permute-start(bf16[64,1536]{1,0:T(8,128)(2,1)S(1)} %collective-permute-done.3), channel_id=1, source_target_pairs={{0,480},{32,0},{64,32},{96,64},{128,96},{160,128},{192,160},{224,1... | collective-permute-start | bytes 589832 | tf_op jit(solution)/shard_map/ppermute | solution.py:19
  88.3 4.5 %collective-permute-done.4 = bf16[64,1536]{1,0:T(8,128)(2,1)S(1)} collective-permute-done((bf16[64,1536]{1,0:T(8,128)(2,1)S(1)}, bf16[64,1536]{1,0:T(8,128)(2,1)S(1)}, u32[]{:S(2)}, u32[]{:S(2)}) %collective-permute-start.4) | collective-permute-done | bytes 196640 | tf_op jit(solution)/shard_map/ppermute | solution.py:16
  94.7 4.6 %collective-permute-start.7 = (bf16[64,1536]{1,0:T(8,128)(2,1)S(1)}, bf16[64,1536]{1,0:T(8,128)(2,1)S(1)}, u32[]{:S(2)}, u32[]{:S(2)}) collective-permute-start(bf16[64,1536]{1,0:T(8,128)(2,1)S(1)} %collective-permute-done.5), channel_id=1, source_target_pairs={{0,480},{32,0},{64,32},{96,64},{128,96},{160,128},{192,160},{224,1... | collective-permute-start | bytes 589832 | tf_op jit(solution)/shard_map/ppermute | solution.py:19
  100.7 4.7 %collective-permute-done.6 = bf16[64,1536]{1,0:T(8,128)(2,1)S(1)} collective-permute-done((bf16[64,1536]{1,0:T(8,128)(2,1)S(1)}, bf16[64,1536]{1,0:T(8,128)(2,1)S(1)}, u32[]{:S(2)}, u32[]{:S(2)}) %collective-permute-start.6) | collective-permute-done | bytes 196640 | tf_op jit(solution)/shard_map/ppermute | solution.py:16
  107.4 4.6 %collective-permute-start.9 = (bf16[64,1536]{1,0:T(8,128)(2,1)S(1)}, bf16[64,1536]{1,0:T(8,128)(2,1)S(1)}, u32[]{:S(2)}, u32[]{:S(2)}) collective-permute-start(bf16[64,1536]{1,0:T(8,128)(2,1)S(1)} %collective-permute-done.7), channel_id=1, source_target_pairs={{0,480},{32,0},{64,32},{96,64},{128,96},{160,128},{192,160},{224,1... | collective-permute-start | bytes 589832 | tf_op jit(solution)/shard_map/ppermute | solution.py:19
  113.3 5.0 %collective-permute-done.8 = bf16[64,1536]{1,0:T(8,128)(2,1)S(1)} collective-permute-done((bf16[64,1536]{1,0:T(8,128)(2,1)S(1)}, bf16[64,1536]{1,0:T(8,128)(2,1)S(1)}, u32[]{:S(2)}, u32[]{:S(2)}) %collective-permute-start.8) | collective-permute-done | bytes 196640 | tf_op jit(solution)/shard_map/ppermute | solution.py:16
  120.3 4.8 %collective-permute-start.11 = (bf16[64,1536]{1,0:T(8,128)(2,1)S(1)}, bf16[64,1536]{1,0:T(8,128)(2,1)S(1)}, u32[]{:S(2)}, u32[]{:S(2)}) collective-permute-start(bf16[64,1536]{1,0:T(8,128)(2,1)S(1)} %collective-permute-done.9), channel_id=1, source_target_pairs={{0,480},{32,0},{64,32},{96,64},{128,96},{160,128},{192,160},{224,1... | collective-permute-start | bytes 589832 | tf_op jit(solution)/shard_map/ppermute | solution.py:19
  125.0 20.0 %all-gather.8.cloned.1.call-done = f32[256,64,128]{2,1,0:T(8,128)} async-done(((f32[16,64,128]{2,1,0:T(8,128)}), f32[256,64,128]{2,1,0:T(8,128)}) %all-gather.8.cloned.1.call-update) | async-done | bytes 8388624 | tf_op jit(solution)/shard_map/all_gather | solution.py:28
  145.1 28.2 %while.9 = (s32[]{:T(128)}, f32[16,64,128]{2,1,0:T(8,128)S(1)}, s32[]{:T(128)}, f32[16,16]{1,0:T(8,128)}, f32[16,16,64,128]{3,2,1,0:T(8,128)}, /*index=5*/s32[]{:T(128)}, s32[]{:T(128)}) while((s32[]{:T(128)}, f32[16,64,128]{2,1,0:T(8,128)S(1)}, s32[]{:T(128)}, f32[16,16]{1,0:T(8,128)}, f32[16,16,64,128]{3,2,1,0:T(8,128)}, ...), condition=%wide.region_4.5_spmd.clone, body=%wide.region_3.4_spmd.clone.sunk | while | flops 524292 | bytes 1573161 | solution.py:37
  186.5 7.5 %all-to-all-start = ((bf16[32,24,1024]{2,1,0:T(8,128)(2,1)}), bf16[32,24,1024]{2,1,0:T(8,128)(2,1)S(1)}, u32[]{:S(2)}, u32[]{:S(2)}) async-start(bf16[32,24,1024]{2,1,0:T(8,128)(2,1)} %bitcast.23), calls=%async_computation | async-start | bytes 3145728 | tf_op jit(solution)/shard_map/all_to_all | solution.py:138
  197.3 4.6 %collective-permute-start.13 = (bf16[64,1536]{1,0:T(8,128)(2,1)S(1)}, bf16[64,1536]{1,0:T(8,128)(2,1)S(1)}, u32[]{:S(2)}, u32[]{:S(2)}) collective-permute-start(bf16[64,1536]{1,0:T(8,128)(2,1)S(1)} %collective-permute-done.11), channel_id=1, source_target_pairs={{0,480},{32,0},{64,32},{96,64},{128,96},{160,128},{192,160},{224,1... | collective-permute-start | bytes 589832 | tf_op jit(solution)/shard_map/ppermute | solution.py:19
  203.3 5.8 %collective-permute-done.12 = bf16[64,1536]{1,0:T(8,128)(2,1)S(1)} collective-permute-done((bf16[64,1536]{1,0:T(8,128)(2,1)S(1)}, bf16[64,1536]{1,0:T(8,128)(2,1)S(1)}, u32[]{:S(2)}, u32[]{:S(2)}) %collective-permute-start.12) | collective-permute-done | bytes 196640 | tf_op jit(solution)/shard_map/ppermute | solution.py:16
  212.4 7.1 %collective-permute-done.14 = bf16[64,1536]{1,0:T(8,128)(2,1)S(1)} collective-permute-done((bf16[64,1536]{1,0:T(8,128)(2,1)S(1)}, bf16[64,1536]{1,0:T(8,128)(2,1)S(1)}, u32[]{:S(2)}, u32[]{:S(2)}) %collective-permute-start.14) | collective-permute-done | bytes 196640 | tf_op jit(solution)/shard_map/ppermute | solution.py:16
  220.2 6.1 %fusion.9 = f32[768,1536]{1,0:T(8,128)} fusion(bf16[768,1024]{1,0:T(8,128)(2,1)S(1)} %bitcast.162, bf16[1,1024,1536]{2,1,0:T(8,128)(2,1)} %all-gather.10.cloned.1.call-done), kind=kOutput, calls=%fused_computation.14 | convolution fusion | flops 2415919104 | bytes 9437184 | tf_op jit(solution)/shard_map/dot_general | solution.py:148
  226.2 62.8 %all-gather.12.cloned.1.call-done = bf16[1,1536,1024]{2,1,0:T(8,128)(2,1)} async-done(((bf16[1,96,1024]{2,1,0:T(8,128)(2,1)}), bf16[1,1536,1024]{2,1,0:T(8,128)(2,1)}) %all-gather.12.cloned.1.call-update) | async-done | bytes 3145744 | tf_op jit(solution)/shard_map/all_gather | solution.py:158
  289.0 10.5 %fusion.16 = bf16[768,1024]{1,0:T(8,128)(2,1)} fusion(bf16[1,1536,1024]{2,1,0:T(8,128)(2,1)} %all-gather.12.cloned.1.call-done, f32[768,1536]{1,0:T(8,128)} %fusion.9, bf16[768,1024]{1,0:T(8,128)(2,1)S(1)} %bitcast.163, bf16[1024,1536]{1,0:T(8,128)(2,1)} %constant_dynamic-update-slice_fusion), kind=kOutput, calls=%fused_computation.21 | convolution fusion | flops 4839702528 | bytes 14155776 | tf_op jit(solution)/shard_map/dot_general | solution.py:156
  299.5 16.2 %all-to-all-start.1 = ((bf16[32,24,1024]{2,1,0:T(8,128)(2,1)}), bf16[32,24,1024]{2,1,0:T(8,128)(2,1)S(1)}, u32[]{:S(2)}, u32[]{:S(2)}) async-start(bf16[32,24,1024]{2,1,0:T(8,128)(2,1)} %bitcast.164), calls=%async_computation.1 | async-start | bytes 3145728 | tf_op jit(solution)/shard_map/all_to_all | solution.py:161
  318.3 20.1 %all-to-all-done.1 = bf16[32,24,1024]{2,1,0:T(8,128)(2,1)S(1)} async-done(((bf16[32,24,1024]{2,1,0:T(8,128)(2,1)}), bf16[32,24,1024]{2,1,0:T(8,128)(2,1)S(1)}, u32[]{:S(2)}, u32[]{:S(2)}) %all-to-all-start.1) | async-done | bytes 1572896 | tf_op jit(solution)/shard_map/all_to_all | solution.py:161
  (152 shorter events, 93.3 us)
Async XLA Ops:
  6.5 47.9 %copy-start = (f32[1,256,128]{2,1,0:T(8,128)S(1)}, f32[1,256,128]{2,1,0:T(8,128)}, u32[]{:S(2)}) copy-start(f32[1,256,128]{2,1,0:T(8,128)} %param.19) | copy-start | bytes 393220
  6.5 138.5 %all-gather.8.cloned.1.call-start = ((), (), s32[]{:S(2)}) async-start(), calls=%async_computation.2 | async-start | bytes 8912896 | tf_op jit(solution)/shard_map/all_gather | solution.py:28
  8.5 18.5 %copy-start.7 = (f32[1,256,16]{1,2,0:T(8,128)S(1)}, f32[1,256,16]{1,2,0:T(8,128)}, u32[]{:S(2)}) copy-start(f32[1,256,16]{1,2,0:T(8,128)} %param.20) | copy-start | bytes 49156
  10.1 17.1 %copy-start.10 = (s32[1,256,2]{1,2,0:T(2,128)S(1)}, s32[1,256,2]{1,2,0:T(2,128)}, u32[]{:S(2)}) copy-start(s32[1,256,2]{1,2,0:T(2,128)} %param.28) | copy-start | bytes 6148
  10.1 44.7 %copy-start.1 = (bf16[1,256,1024]{2,1,0:T(8,128)(2,1)S(1)}, bf16[1,256,1024]{2,1,0:T(8,128)(2,1)}, u32[]{:S(2)}) copy-start(bf16[1,256,1024]{2,1,0:T(8,128)(2,1)} %param.17) | copy-start | bytes 1572868
  12.0 208.2 %all-gather.10.cloned.1.call-start = ((), (), s32[]{:S(2)}) async-start(), calls=%async_computation.3 | async-start | bytes 3342336 | tf_op jit(solution)/shard_map/all_gather | solution.py:150
  12.8 276.3 %all-gather.12.cloned.1.call-start = ((), (), s32[]{:S(2)}) async-start(), calls=%async_computation.4 | async-start | bytes 3342336 | tf_op jit(solution)/shard_map/all_gather | solution.py:158
  12.8 55.4 %collective-permute-start = (bf16[64,1536]{1,0:T(8,128)(2,1)S(1)}, bf16[64,1536]{1,0:T(8,128)(2,1)S(1)}, u32[]{:S(2)}, u32[]{:S(2)}) collective-permute-start(bf16[64,1536]{1,0:T(8,128)(2,1)S(1)} %bitcast.167), channel_id=1, source_target_pairs={{0,32},{32,64},{64,96},{96,128},{128,160},{160,192},{192,224},{224... | collective-permute-start | bytes 589832 | tf_op jit(solution)/shard_map/ppermute | solution.py:16
  17.2 52.9 %collective-permute-start.1 = (bf16[64,1536]{1,0:T(8,128)(2,1)S(1)}, bf16[64,1536]{1,0:T(8,128)(2,1)S(1)}, u32[]{:S(2)}, u32[]{:S(2)}) collective-permute-start(bf16[64,1536]{1,0:T(8,128)(2,1)S(1)} %bitcast.168), channel_id=1, source_target_pairs={{0,480},{32,0},{64,32},{96,64},{128,96},{160,128},{192,160},{224,1... | collective-permute-start | bytes 589832 | tf_op jit(solution)/shard_map/ppermute | solution.py:19
  68.2 12.2 %collective-permute-start.2 = (bf16[64,1536]{1,0:T(8,128)(2,1)S(1)}, bf16[64,1536]{1,0:T(8,128)(2,1)S(1)}, u32[]{:S(2)}, u32[]{:S(2)}) collective-permute-start(bf16[64,1536]{1,0:T(8,128)(2,1)S(1)} %collective-permute-done), channel_id=1, source_target_pairs={{0,32},{32,64},{64,96},{96,128},{128,160},{160,192},{192,224},{224... | collective-permute-start | bytes 589832 | tf_op jit(solution)/shard_map/ppermute | solution.py:16
  70.1 12.2 %collective-permute-start.3 = (bf16[64,1536]{1,0:T(8,128)(2,1)S(1)}, bf16[64,1536]{1,0:T(8,128)(2,1)S(1)}, u32[]{:S(2)}, u32[]{:S(2)}) collective-permute-start(bf16[64,1536]{1,0:T(8,128)(2,1)S(1)} %collective-permute-done.1), channel_id=1, source_target_pairs={{0,480},{32,0},{64,32},{96,64},{128,96},{160,128},{192,160},{224,1... | collective-permute-start | bytes 589832 | tf_op jit(solution)/shard_map/ppermute | solution.py:19
  80.4 12.4 %collective-permute-start.4 = (bf16[64,1536]{1,0:T(8,128)(2,1)S(1)}, bf16[64,1536]{1,0:T(8,128)(2,1)S(1)}, u32[]{:S(2)}, u32[]{:S(2)}) collective-permute-start(bf16[64,1536]{1,0:T(8,128)(2,1)S(1)} %collective-permute-done.2), channel_id=1, source_target_pairs={{0,32},{32,64},{64,96},{96,128},{128,160},{160,192},{192,224},{224... | collective-permute-start | bytes 589832 | tf_op jit(solution)/shard_map/ppermute | solution.py:16
  82.3 12.4 %collective-permute-start.5 = (bf16[64,1536]{1,0:T(8,128)(2,1)S(1)}, bf16[64,1536]{1,0:T(8,128)(2,1)S(1)}, u32[]{:S(2)}, u32[]{:S(2)}) collective-permute-start(bf16[64,1536]{1,0:T(8,128)(2,1)S(1)} %collective-permute-done.3), channel_id=1, source_target_pairs={{0,480},{32,0},{64,32},{96,64},{128,96},{160,128},{192,160},{224,1... | collective-permute-start | bytes 589832 | tf_op jit(solution)/shard_map/ppermute | solution.py:19
  92.8 12.7 %collective-permute-start.6 = (bf16[64,1536]{1,0:T(8,128)(2,1)S(1)}, bf16[64,1536]{1,0:T(8,128)(2,1)S(1)}, u32[]{:S(2)}, u32[]{:S(2)}) collective-permute-start(bf16[64,1536]{1,0:T(8,128)(2,1)S(1)} %collective-permute-done.4), channel_id=1, source_target_pairs={{0,32},{32,64},{64,96},{96,128},{128,160},{160,192},{192,224},{224... | collective-permute-start | bytes 589832 | tf_op jit(solution)/shard_map/ppermute | solution.py:16
  94.7 12.6 %collective-permute-start.7 = (bf16[64,1536]{1,0:T(8,128)(2,1)S(1)}, bf16[64,1536]{1,0:T(8,128)(2,1)S(1)}, u32[]{:S(2)}, u32[]{:S(2)}) collective-permute-start(bf16[64,1536]{1,0:T(8,128)(2,1)S(1)} %collective-permute-done.5), channel_id=1, source_target_pairs={{0,480},{32,0},{64,32},{96,64},{128,96},{160,128},{192,160},{224,1... | collective-permute-start | bytes 589832 | tf_op jit(solution)/shard_map/ppermute | solution.py:19
  105.4 12.9 %collective-permute-start.8 = (bf16[64,1536]{1,0:T(8,128)(2,1)S(1)}, bf16[64,1536]{1,0:T(8,128)(2,1)S(1)}, u32[]{:S(2)}, u32[]{:S(2)}) collective-permute-start(bf16[64,1536]{1,0:T(8,128)(2,1)S(1)} %collective-permute-done.6), channel_id=1, source_target_pairs={{0,32},{32,64},{64,96},{96,128},{128,160},{160,192},{192,224},{224... | collective-permute-start | bytes 589832 | tf_op jit(solution)/shard_map/ppermute | solution.py:16
  107.4 12.9 %collective-permute-start.9 = (bf16[64,1536]{1,0:T(8,128)(2,1)S(1)}, bf16[64,1536]{1,0:T(8,128)(2,1)S(1)}, u32[]{:S(2)}, u32[]{:S(2)}) collective-permute-start(bf16[64,1536]{1,0:T(8,128)(2,1)S(1)} %collective-permute-done.7), channel_id=1, source_target_pairs={{0,480},{32,0},{64,32},{96,64},{128,96},{160,128},{192,160},{224,1... | collective-permute-start | bytes 589832 | tf_op jit(solution)/shard_map/ppermute | solution.py:19
  118.4 77.0 %collective-permute-start.10 = (bf16[64,1536]{1,0:T(8,128)(2,1)S(1)}, bf16[64,1536]{1,0:T(8,128)(2,1)S(1)}, u32[]{:S(2)}, u32[]{:S(2)}) collective-permute-start(bf16[64,1536]{1,0:T(8,128)(2,1)S(1)} %collective-permute-done.8), channel_id=1, source_target_pairs={{0,32},{32,64},{64,96},{96,128},{128,160},{160,192},{192,224},{224... | collective-permute-start | bytes 589832 | tf_op jit(solution)/shard_map/ppermute | solution.py:16
  120.3 77.0 %collective-permute-start.11 = (bf16[64,1536]{1,0:T(8,128)(2,1)S(1)}, bf16[64,1536]{1,0:T(8,128)(2,1)S(1)}, u32[]{:S(2)}, u32[]{:S(2)}) collective-permute-start(bf16[64,1536]{1,0:T(8,128)(2,1)S(1)} %collective-permute-done.9), channel_id=1, source_target_pairs={{0,480},{32,0},{64,32},{96,64},{128,96},{160,128},{192,160},{224,1... | collective-permute-start | bytes 589832 | tf_op jit(solution)/shard_map/ppermute | solution.py:19
  186.5 33.7 %all-to-all-start = ((bf16[32,24,1024]{2,1,0:T(8,128)(2,1)}), bf16[32,24,1024]{2,1,0:T(8,128)(2,1)S(1)}, u32[]{:S(2)}, u32[]{:S(2)}) async-start(bf16[32,24,1024]{2,1,0:T(8,128)(2,1)} %bitcast.23), calls=%async_computation | async-start | bytes 3145728 | tf_op jit(solution)/shard_map/all_to_all | solution.py:138
  195.4 13.7 %collective-permute-start.12 = (bf16[64,1536]{1,0:T(8,128)(2,1)S(1)}, bf16[64,1536]{1,0:T(8,128)(2,1)S(1)}, u32[]{:S(2)}, u32[]{:S(2)}) collective-permute-start(bf16[64,1536]{1,0:T(8,128)(2,1)S(1)} %collective-permute-done.10), channel_id=1, source_target_pairs={{0,32},{32,64},{64,96},{96,128},{128,160},{160,192},{192,224},{224... | collective-permute-start | bytes 589832 | tf_op jit(solution)/shard_map/ppermute | solution.py:16
  197.3 14.4 %collective-permute-start.13 = (bf16[64,1536]{1,0:T(8,128)(2,1)S(1)}, bf16[64,1536]{1,0:T(8,128)(2,1)S(1)}, u32[]{:S(2)}, u32[]{:S(2)}) collective-permute-start(bf16[64,1536]{1,0:T(8,128)(2,1)S(1)} %collective-permute-done.11), channel_id=1, source_target_pairs={{0,480},{32,0},{64,32},{96,64},{128,96},{160,128},{192,160},{224,1... | collective-permute-start | bytes 589832 | tf_op jit(solution)/shard_map/ppermute | solution.py:19
  209.1 10.4 %collective-permute-start.14 = (bf16[64,1536]{1,0:T(8,128)(2,1)S(1)}, bf16[64,1536]{1,0:T(8,128)(2,1)S(1)}, u32[]{:S(2)}, u32[]{:S(2)}) collective-permute-start(bf16[64,1536]{1,0:T(8,128)(2,1)S(1)} %collective-permute-done.12), channel_id=1, source_target_pairs={{0,32},{32,64},{64,96},{96,128},{128,160},{160,192},{192,224},{224... | collective-permute-start | bytes 589832 | tf_op jit(solution)/shard_map/ppermute | solution.py:16
  299.5 38.9 %all-to-all-start.1 = ((bf16[32,24,1024]{2,1,0:T(8,128)(2,1)}), bf16[32,24,1024]{2,1,0:T(8,128)(2,1)S(1)}, u32[]{:S(2)}, u32[]{:S(2)}) async-start(bf16[32,24,1024]{2,1,0:T(8,128)(2,1)} %bitcast.164), calls=%async_computation.1 | async-start | bytes 3145728 | tf_op jit(solution)/shard_map/all_to_all | solution.py:161
  (11 other events, 55.0 us)
Sparse Core Ops, SparseCore 0:
  12.1 132.8 all-gather.7
  147.1 68.2 all-gather.9
  217.5 71.5 all-gather.11
